TPU v7x, 32 devices: a whole 2x2x4 slice. The times are simulated.
32 devices in a mesh: tm: 16 (over z, y, x), col: 2 (over core).
Axes of the slice: x: 2, y: 2, z: 4, core: 2. Of those that a mesh axis runs over, the one named last changes fastest.
Arguments:
- rhs: float32 [16, 1024, 256], P('tm', 'col'), may hold values from -6 to 6
- inverse_blocks: float32 [3, 16, 1024, 1024], P(None, 'tm', None, 'col'), may hold values from -2 to 3, as said below
- lower_coupling: float32 [3, 16, 1024, 1024], P(None, 'tm', None, 'col'), may hold values from -0.1875 to 0.1875
- upper_coupling: float32 [3, 16, 1024, 1024], P(None, 'tm', None, 'col'), may hold values from -0.1875 to 0.1875
- tile_pattern: int32 [3, 16, 2, 8, 8], P(None, 'tm', None, None, 'col'), may hold values from 0 to 1, as said below
- tip_coupling: float32 [3, 16, 64, 1024], P(None, 'tm', None, 'col'), may hold values from -0.046875 to 0.046875
- tip_rhs: float32 [64, 256], replicated, may hold values from -6 to 6
Outputs:
- reduced: float32 [16, 1024, 256], P('tm', 'col')
- tip_reduced: float32 [64, 256], replicated
Inputs may be any that keep to these rules, and one draw needn't show every extreme that they name: Every inverse_blocks[l, j] is symmetric. tile_pattern[l, j, k, r, c] is 1 exactly where |r - c| is at most a half-width w[l, j, k] of 1 to 4; both half-widths 1 and 4 occur.
All inputs are finite; a program needn't handle non-finite values.
Results may differ from a plain program's by a relative error of at most 0.0001.
Values sent between devices are 32-bit elements; how exact they have to be, the bound alone decides.
A program may use at most 64 MiB of HBM per device.

v0:
```python
import jax
import jax.numpy as jnp
from jax import lax
from jax.sharding import PartitionSpec as P


def passed_along(block, axis, distance):
    devices = range(lax.axis_size(axis))
    route = [((i - distance) % len(devices), i) for i in devices]
    return lax.ppermute(block, axis, route)


def local(rhs, inverse_blocks, lower_coupling, upper_coupling, tile_pattern, tip_coupling, tip_rhs):
    highest = lax.Precision.HIGHEST
    own_cols = inverse_blocks.shape[3]
    block_order = inverse_blocks.shape[2]
    tiles_here = tile_pattern.shape[4]
    tiles_all = tile_pattern.shape[3]
    tile_size = block_order // tiles_all
    level_count = inverse_blocks.shape[0]

    def apply_pattern(coupling, pattern):
        reshaped_rows = coupling.reshape(tiles_all, tile_size, tiles_here, tile_size)
        masked = reshaped_rows * pattern.astype(jnp.float32)[:, None, :, None]
        return masked.reshape(block_order, own_cols)

    present_rows = rhs[0]
    pending = jnp.zeros(tip_rhs.shape, jnp.float32)
    for level_number in range(level_count):
        stride = 2**level_number
        lower_masked = apply_pattern(
            lower_coupling[level_number, 0], tile_pattern[level_number, 0, 0]
        )
        upper_masked = apply_pattern(
            upper_coupling[level_number, 0], tile_pattern[level_number, 0, 1]
        )
        inverse = inverse_blocks[level_number, 0]

        def row_term(first_row, row_count, input_rows=present_rows, inverse_here=inverse):
            return jnp.dot(
                inverse_here, input_rows, precision=highest, preferred_element_type=jnp.float32
            )

        solved = lax.psum_scatter(
            row_term(jnp.int32(0), own_cols * lax.axis_size("col")),
            "col",
            scatter_dimension=0,
            tiled=True,
        )
        whole_solved = lax.all_gather(solved, "col", axis=0, tiled=True)
        down_term = jnp.dot(
            lower_masked.T, whole_solved, precision=highest, preferred_element_type=jnp.float32
        )
        up_term = jnp.dot(
            upper_masked.T, whole_solved, precision=highest, preferred_element_type=jnp.float32
        )
        from_above = passed_along(down_term, "tm", -stride)
        from_below = passed_along(up_term, "tm", stride)
        present_rows = present_rows - from_above - from_below
        arrow_part = jnp.dot(
            tip_coupling[level_number, 0],
            solved,
            precision=highest,
            preferred_element_type=jnp.float32,
        )
        pending = pending + arrow_part
    tip_total = tip_rhs - lax.psum(pending, ("tm", "col"))
    return (present_rows[None], tip_total)


def solution(mesh):
    return jax.shard_map(
        local,
        mesh=mesh,
        in_specs=(
            P("tm", "col", None),
            P(None, "tm", None, "col"),
            P(None, "tm", None, "col"),
            P(None, "tm", None, "col"),
            P(None, "tm", None, None, "col"),
            P(None, "tm", None, "col"),
            P(),
        ),
        out_specs=(P("tm", "col", None), P()),
        check_vma=False,
    )
```

profile of v0, /device:TPU:1, one launch (start us, length us, event | category | flops | bytes accessed | tf_op | source)
XLA Modules:
  0.0 310.0 jit_solution(16763351207113429849)
XLA Ops:
  7.2 4.5 %fusion.21 = f32[1024,256]{1,0:T(8,128)} fusion(f32[3,1,1024,512]{3,2,1,0:T(8,128)} %param.8, f32[1,512,256]{2,1,0:T(8,128)} %param.7), kind=kOutput, calls=%fused_computation.27 | convolution fusion | flops 1610612736 | bytes 3670016 | tf_op jit(solution)/shard_map/dot_general | solution.py:40
  11.8 11.0 %reduce-scatter.4.cloned.1.call-done = f32[512,256]{1,0:T(8,128)} async-done(((f32[1024,256]{1,0:T(8,128)}), f32[512,256]{1,0:T(8,128)}) %reduce-scatter.4.cloned.1.call-update) | async-done | bytes 524304 | tf_op jit(solution)/shard_map/reduce_scatter | solution.py:44
  23.0 11.5 %all-gather.4.cloned.1.call-done = f32[1024,256]{1,0:T(8,128)} async-done(((f32[512,256]{1,0:T(8,128)}), f32[1024,256]{1,0:T(8,128)}) %all-gather.4.cloned.1.call-update) | async-done | bytes 1048592 | tf_op jit(solution)/shard_map/all_gather | solution.py:50
  35.8 5.1 %fusion.10 = f32[512,256]{1,0:T(8,128)S(1)} fusion(f32[1024,256]{1,0:T(8,128)S(1)} %copy-done, f32[128,8,4,128]{3,2,1,0:T(4,128)S(1)} %bitcast.121, f32[3,1,1024,512]{3,2,1,0:T(8,128)} %param.9), kind=kOutput, calls=%fused_computation.16 | convolution fusion | flops 1611137024 | bytes 5767168 | tf_op jit(solution)/shard_map/dot_general | solution.py:51
  40.8 5.3 %collective-permute-start = (f32[512,256]{1,0:T(8,128)S(1)}, f32[512,256]{1,0:T(8,128)S(1)}, u32[]{:S(2)}, u32[]{:S(2)}) collective-permute-start(f32[512,256]{1,0:T(8,128)S(1)} %fusion.10), channel_id=1, source_target_pairs={{2,0},{4,2},{6,4},{8,6},{10,8},{12,10},{14,12},{16,14},{18,16},{20... | collective-permute-start | bytes 1572872 | tf_op jit(solution)/shard_map/ppermute | solution.py:10
  46.4 5.1 %fusion.8 = f32[512,256]{1,0:T(8,128)S(1)} fusion(f32[1024,256]{1,0:T(8,128)S(1)} %copy-done, f32[128,8,4,128]{3,2,1,0:T(4,128)S(1)} %bitcast.118, f32[3,1,1024,512]{3,2,1,0:T(8,128)} %param.10), kind=kOutput, calls=%fused_computation.13 | convolution fusion | flops 1611137024 | bytes 5767168 | tf_op jit(solution)/shard_map/dot_general | solution.py:54
  51.8 5.3 %collective-permute-done = f32[512,256]{1,0:T(8,128)S(1)} collective-permute-done((f32[512,256]{1,0:T(8,128)S(1)}, f32[512,256]{1,0:T(8,128)S(1)}, u32[]{:S(2)}, u32[]{:S(2)}) %collective-permute-start) | collective-permute-done | bytes 524320 | tf_op jit(solution)/shard_map/ppermute | solution.py:10
  57.1 11.2 %collective-permute-done.1 = f32[512,256]{1,0:T(8,128)S(1)} collective-permute-done((f32[512,256]{1,0:T(8,128)S(1)}, f32[512,256]{1,0:T(8,128)S(1)}, u32[]{:S(2)}, u32[]{:S(2)}) %collective-permute-start.1) | collective-permute-done | bytes 524320 | tf_op jit(solution)/shard_map/ppermute | solution.py:10
  68.5 6.1 %fusion.33 = f32[1024,256]{0,1:T(8,128)} fusion(f32[512,256]{1,0:T(8,128)S(1)} %fusion.41, f32[3,1,1024,512]{3,2,1,0:T(8,128)} %param.8), kind=kOutput, calls=%fused_computation.39 | convolution fusion | flops 1610612736 | bytes 3670016 | tf_op jit(solution)/shard_map/dot_general | solution.py:40
  74.7 10.2 %reduce-scatter.6.cloned.1.call-done = f32[512,256]{0,1:T(8,128)} async-done(((f32[1024,256]{0,1:T(8,128)}), f32[512,256]{0,1:T(8,128)}) %reduce-scatter.6.cloned.1.call-update) | async-done | bytes 524304 | tf_op jit(solution)/shard_map/reduce_scatter | solution.py:44
  85.1 11.4 %all-gather.6.cloned.1.call-done = f32[1024,256]{0,1:T(8,128)} async-done(((f32[512,256]{0,1:T(8,128)}), f32[1024,256]{0,1:T(8,128)}) %all-gather.6.cloned.1.call-update) | async-done | bytes 1048592 | tf_op jit(solution)/shard_map/all_gather | solution.py:50
  97.7 5.0 %fusion.6 = f32[512,256]{1,0:T(8,128)S(1)} fusion(f32[1024,256]{0,1:T(8,128)S(1)} %copy-done.2, f32[128,8,4,128]{3,2,1,0:T(4,128)S(1)} %bitcast.122, f32[3,1,1024,512]{3,2,1,0:T(8,128)} %param.9), kind=kOutput, calls=%fused_computation.10 | convolution fusion | flops 1611137024 | bytes 5767168 | tf_op jit(solution)/shard_map/dot_general | solution.py:51
  102.8 4.4 %collective-permute-start.2 = (f32[512,256]{1,0:T(8,128)S(1)}, f32[512,256]{1,0:T(8,128)S(1)}, u32[]{:S(2)}, u32[]{:S(2)}) collective-permute-start(f32[512,256]{1,0:T(8,128)S(1)} %fusion.6), channel_id=1, source_target_pairs={{4,0},{6,2},{8,4},{10,6},{12,8},{14,10},{16,12},{18,14},{20,16},{2... | collective-permute-start | bytes 1572872 | tf_op jit(solution)/shard_map/ppermute | solution.py:10
  107.5 5.0 %fusion.4 = f32[512,256]{1,0:T(8,128)S(1)} fusion(f32[1024,256]{0,1:T(8,128)S(1)} %copy-done.2, f32[128,8,4,128]{3,2,1,0:T(4,128)S(1)} %bitcast.119, f32[3,1,1024,512]{3,2,1,0:T(8,128)} %param.10), kind=kOutput, calls=%fused_computation.7 | convolution fusion | flops 1611137024 | bytes 5767168 | tf_op jit(solution)/shard_map/dot_general | solution.py:54
  112.8 5.4 %collective-permute-done.2 = f32[512,256]{1,0:T(8,128)S(1)} collective-permute-done((f32[512,256]{1,0:T(8,128)S(1)}, f32[512,256]{1,0:T(8,128)S(1)}, u32[]{:S(2)}, u32[]{:S(2)}) %collective-permute-start.2) | collective-permute-done | bytes 524320 | tf_op jit(solution)/shard_map/ppermute | solution.py:10
  118.2 10.3 %collective-permute-done.3 = f32[512,256]{1,0:T(8,128)S(1)} collective-permute-done((f32[512,256]{1,0:T(8,128)S(1)}, f32[512,256]{1,0:T(8,128)S(1)}, u32[]{:S(2)}, u32[]{:S(2)}) %collective-permute-start.3) | collective-permute-done | bytes 524320 | tf_op jit(solution)/shard_map/ppermute | solution.py:10
  128.5 6.1 %fusion.36 = f32[1024,256]{0,1:T(8,128)} fusion(f32[3,1,1024,512]{3,2,1,0:T(8,128)} %param.8, f32[512,256]{1,0:T(8,128)S(1)} %collective-permute-done.3, f32[512,256]{1,0:T(8,128)S(1)} %fusion.41, f32[512,256]{1,0:T(8,128)S(1)} %collective-permute-done.2), kind=kOutput, calls=%fused_computation.40 | convolution fusion | flops 1610874880 | bytes 4718592 | tf_op jit(solution)/shard_map/dot_general | solution.py:40
  134.7 12.1 %reduce-scatter.8.cloned.1.call-done = f32[512,256]{0,1:T(8,128)} async-done(((f32[1024,256]{0,1:T(8,128)}), f32[512,256]{0,1:T(8,128)}) %reduce-scatter.8.cloned.1.call-update) | async-done | bytes 524304 | tf_op jit(solution)/shard_map/reduce_scatter | solution.py:44
  147.0 11.4 %all-gather.8.cloned.1.call-done = f32[1024,256]{0,1:T(8,128)} async-done(((f32[512,256]{0,1:T(8,128)}), f32[1024,256]{0,1:T(8,128)}) %all-gather.8.cloned.1.call-update) | async-done | bytes 1048592 | tf_op jit(solution)/shard_map/all_gather | solution.py:50
  159.6 5.0 %fusion.2 = f32[512,256]{1,0:T(8,128)S(1)} fusion(f32[1024,256]{0,1:T(8,128)S(1)} %copy-done.1, f32[128,8,4,128]{3,2,1,0:T(4,128)S(1)} %bitcast.123, f32[3,1,1024,512]{3,2,1,0:T(8,128)} %param.9), kind=kOutput, calls=%fused_computation.4 | convolution fusion | flops 1611137024 | bytes 5767168 | tf_op jit(solution)/shard_map/dot_general | solution.py:51
  164.7 3.4 %collective-permute-start.4 = (f32[512,256]{1,0:T(8,128)S(1)}, f32[512,256]{1,0:T(8,128)S(1)}, u32[]{:S(2)}, u32[]{:S(2)}) collective-permute-start(f32[512,256]{1,0:T(8,128)S(1)} %fusion.2), channel_id=1, source_target_pairs={{8,0},{10,2},{12,4},{14,6},{16,8},{18,10},{20,12},{22,14},{24,16},... | collective-permute-start | bytes 1572872 | tf_op jit(solution)/shard_map/ppermute | solution.py:10
  168.5 6.0 %fusion = f32[512,256]{1,0:T(8,128)} fusion(f32[1024,256]{0,1:T(8,128)S(1)} %copy-done.1, f32[128,8,4,128]{3,2,1,0:T(4,128)S(1)} %bitcast.120, f32[3,1,1024,512]{3,2,1,0:T(8,128)} %param.10), kind=kOutput, calls=%fused_computation.1 | convolution fusion | flops 1611137024 | bytes 5767168 | tf_op jit(solution)/shard_map/dot_general | solution.py:54
  176.8 123.9 %all-reduce.2.cloned.1.call-done = f32[64,256]{1,0:T(8,128)} async-done(((f32[64,256]{1,0:T(8,128)}), f32[64,256]{1,0:T(8,128)}) %all-reduce.2.cloned.1.call-update) | async-done | bytes 65552 | tf_op jit(solution)/shard_map/psum | solution.py:67
  300.7 1.5 sub.27
  (57 shorter events, 9.4 us)
Async XLA Ops:
  7.2 15.7 %copy-start.9 = (s32[3,1,2,8,4]{3,4,2,1,0:T(4,128)S(1)}, s32[3,1,2,8,4]{3,4,2,1,0:T(4,128)}, u32[]{:S(2)}) copy-start(s32[3,1,2,8,4]{3,4,2,1,0:T(4,128)} %param.11) | copy-start | bytes 2308
  7.2 15.6 %reduce-scatter.4.cloned.1.call-start = ((), (), s32[]{:S(2)}) async-start(), calls=%async_computation.3 | async-start | bytes 1572864 | tf_op jit(solution)/shard_map/reduce_scatter | solution.py:44
  11.7 22.8 %all-gather.4.cloned.1.call-start = ((), (), s32[]{:S(2)}) async-start(), calls=%async_computation.4 | async-start | bytes 1572864 | tf_op jit(solution)/shard_map/all_gather | solution.py:50
  22.8 62.1 %reduce-scatter.6.cloned.1.call-start = ((), (), s32[]{:S(2)}) async-start(), calls=%async_computation.5 | async-start | bytes 1572864 | tf_op jit(solution)/shard_map/reduce_scatter | solution.py:44
  34.5 1.2 copy-start
  40.8 16.3 %collective-permute-start = (f32[512,256]{1,0:T(8,128)S(1)}, f32[512,256]{1,0:T(8,128)S(1)}, u32[]{:S(2)}, u32[]{:S(2)}) collective-permute-start(f32[512,256]{1,0:T(8,128)S(1)} %fusion.10), channel_id=1, source_target_pairs={{2,0},{4,2},{6,4},{8,6},{10,8},{12,10},{14,12},{16,14},{18,16},{20... | collective-permute-start | bytes 1572872 | tf_op jit(solution)/shard_map/ppermute | solution.py:10
  46.4 21.9 %copy-start.3 = (f32[1,512,256]{2,1,0:T(8,128)S(1)}, f32[1,512,256]{2,1,0:T(8,128)}, u32[]{:S(2)}) copy-start(f32[1,512,256]{2,1,0:T(8,128)} %param.7) | copy-start | bytes 1572868
  51.6 16.8 %collective-permute-start.1 = (f32[512,256]{1,0:T(8,128)S(1)}, f32[512,256]{1,0:T(8,128)S(1)}, u32[]{:S(2)}, u32[]{:S(2)}) collective-permute-start(f32[512,256]{1,0:T(8,128)S(1)} %fusion.8), channel_id=1, source_target_pairs={{30,0},{0,2},{2,4},{4,6},{6,8},{8,10},{10,12},{12,14},{14,16},{16,... | collective-permute-start | bytes 1572872 | tf_op jit(solution)/shard_map/ppermute | solution.py:10
  74.6 21.9 %all-gather.6.cloned.1.call-start = ((), (), s32[]{:S(2)}) async-start(), calls=%async_computation.6 | async-start | bytes 1572864 | tf_op jit(solution)/shard_map/all_gather | solution.py:50
  84.9 61.9 %reduce-scatter.8.cloned.1.call-start = ((), (), s32[]{:S(2)}) async-start(), calls=%async_computation.7 | async-start | bytes 1572864 | tf_op jit(solution)/shard_map/reduce_scatter | solution.py:44
  96.5 1.2 copy-start.2
  102.8 15.4 %collective-permute-start.2 = (f32[512,256]{1,0:T(8,128)S(1)}, f32[512,256]{1,0:T(8,128)S(1)}, u32[]{:S(2)}, u32[]{:S(2)}) collective-permute-start(f32[512,256]{1,0:T(8,128)S(1)} %fusion.6), channel_id=1, source_target_pairs={{4,0},{6,2},{8,4},{10,6},{12,8},{14,10},{16,12},{18,14},{20,16},{2... | collective-permute-start | bytes 1572872 | tf_op jit(solution)/shard_map/ppermute | solution.py:10
  112.5 16.0 %collective-permute-start.3 = (f32[512,256]{1,0:T(8,128)S(1)}, f32[512,256]{1,0:T(8,128)S(1)}, u32[]{:S(2)}, u32[]{:S(2)}) collective-permute-start(f32[512,256]{1,0:T(8,128)S(1)} %fusion.4), channel_id=1, source_target_pairs={{28,0},{30,2},{0,4},{2,6},{4,8},{6,10},{8,12},{10,14},{12,16},{14,... | collective-permute-start | bytes 1572872 | tf_op jit(solution)/shard_map/ppermute | solution.py:10
  134.7 23.7 %all-gather.8.cloned.1.call-start = ((), (), s32[]{:S(2)}) async-start(), calls=%async_computation.8 | async-start | bytes 1572864 | tf_op jit(solution)/shard_map/all_gather | solution.py:50
  146.8 153.9 %all-reduce.2.cloned.1.call-start = ((), (), s32[]{:S(2)}) async-start(), calls=%async_computation.9 | async-start | bytes 131072 | tf_op jit(solution)/shard_map/psum | solution.py:67
  158.4 1.2 copy-start.1
  164.7 137.5 %collective-permute-start.4 = (f32[512,256]{1,0:T(8,128)S(1)}, f32[512,256]{1,0:T(8,128)S(1)}, u32[]{:S(2)}, u32[]{:S(2)}) collective-permute-start(f32[512,256]{1,0:T(8,128)S(1)} %fusion.2), channel_id=1, source_target_pairs={{8,0},{10,2},{12,4},{14,6},{16,8},{18,10},{20,12},{22,14},{24,16},... | collective-permute-start | bytes 1572872 | tf_op jit(solution)/shard_map/ppermute | solution.py:10
  168.4 6.0 %copy-start.4 = (f32[512,256]{1,0:T(8,128)S(1)}, f32[512,256]{1,0:T(8,128)}, u32[]{:S(2)}) copy-start(f32[512,256]{1,0:T(8,128)} %reduce-scatter.4.cloned.1.call-done) | copy-start | bytes 1572868
  168.5 6.0 %copy-start.7 = (f32[3,1,64,512]{3,2,1,0:T(8,128)S(1)}, f32[3,1,64,512]{3,2,1,0:T(8,128)}, u32[]{:S(2)}) copy-start(f32[3,1,64,512]{3,2,1,0:T(8,128)} %param.12) | copy-start | bytes 1179652
  168.5 6.4 %copy-start.5 = (f32[512,256]{0,1:T(8,128)S(1)}, f32[512,256]{0,1:T(8,128)}, u32[]{:S(2)}) copy-start(f32[512,256]{0,1:T(8,128)} %reduce-scatter.6.cloned.1.call-done) | copy-start | bytes 1572868
  168.5 7.1 %copy-start.6 = (f32[512,256]{0,1:T(8,128)S(1)}, f32[512,256]{0,1:T(8,128)}, u32[]{:S(2)}) copy-start(f32[512,256]{0,1:T(8,128)} %reduce-scatter.8.cloned.1.call-done) | copy-start | bytes 1572868
  174.5 126.2 %copy-start.8 = (f32[64,256]{1,0:T(8,128)S(1)}, f32[64,256]{1,0:T(8,128)}, u32[]{:S(2)}) copy-start(f32[64,256]{1,0:T(8,128)} %param.13) | copy-start | bytes 196612
  174.5 127.7 %collective-permute-start.5 = (f32[512,256]{1,0:T(8,128)}, f32[512,256]{1,0:T(8,128)S(1)}, u32[]{:S(2)}, u32[]{:S(2)}) collective-permute-start(f32[512,256]{1,0:T(8,128)} %fusion), channel_id=1, source_target_pairs={{24,0},{26,2},{28,4},{30,6},{0,8},{2,10},{4,12},{6,14},{8,16},{10,... | collective-permute-start | bytes 1572872 | tf_op jit(solution)/shard_map/ppermute | solution.py:10
Sparse Core Ops, SparseCore 0:
  11.9 10.8 reduce-scatter.3
  24.3 10.1 all-gather.3
  74.7 10.0 reduce-scatter.5
  86.3 10.2 all-gather.5
  134.8 11.9 reduce-scatter.7
  148.2 10.1 all-gather.7
  176.9 123.6 all-reduce.1
where the time goes:
time: 310 us
  waiting for transfers between devices  224 us (72%)
  matrix products  50.3 us (16%)
  between operations  14.3 us (5%)
  starting transfers between devices  13.8 us (4%)
  local copies, waits for them, and re-layouts  5.17 us (2%)
    psum x1, waiting for transfers between devices, local(): tip_total = tip_rhs - lax.psum(pending, ('tm', 'col'))  124 us
    all_gather x3, waiting for transfers between devices, local(): whole_solved = lax.all_gather(solved, 'col', axis=0, tiled=True)  34.3 us
    reduce_scatter x3, waiting for transfers between devices, local(): lax.psum_scatter(row_term(jnp.int32(0), own_cols * lax.axis_size('col')),...  33.3 us
    ppermute x6, waiting for transfers between devices, passed_along(): return lax.ppermute(block, axis, route)  32.2 us
    dot_general x3, matrix products, row_term(): jnp.dot(inverse_here, input_rows, precision=highest, preferred_element_ty...  16.7 us
    dot_general x3, matrix products, local(): jnp.dot(upper_masked.T, whole_solved, precision=highest, preferred_elemen...  16.1 us
    dot_general x3, matrix products, local(): jnp.dot(lower_masked.T, whole_solved, precision=highest, preferred_elemen...  15.1 us
    ppermute x6, starting transfers between devices, passed_along(): return lax.ppermute(block, axis, route)  13.6 us
  transfers between devices with their start and end apart: 13, of which 11 were waited for; matrix products, arithmetic and copies ran while one was open for 7% of the time, Pallas kernels for 0%

commit v1 on v0

--- a/solution.py
+++ b/solution.py
@@ -64,7 +64,7 @@
             preferred_element_type=jnp.float32,
         )
         pending = pending + arrow_part
-    tip_total = tip_rhs - lax.psum(pending, ("tm", "col"))
+    tip_total = tip_rhs - jnp.sum(lax.all_gather(pending, ("tm", "col")), axis=0)
     return (present_rows[None], tip_total)
 
 

time: 310 us -> 237 us (0.76)
  waiting for transfers between devices: 224 us -> 150 us
    psum x1 -> x0, waiting for transfers between devices: 124 us -> none  [local(): tip_total = tip_rhs - lax.psum(pending, ('tm', 'col'))]
    all_gather x0 -> x1, waiting for transfers between devices: none -> 33 us  [local(): lax.all_gather(pending, ('tm', 'col'))]
    ppermute x6, waiting for transfers between devices: 32.2 us -> 51.4 us  [passed_along(): return lax.ppermute(block, axis, route)]
  transfers between devices with their start and end apart: 13 -> 13, of which waited for: 11 -> 13; matrix products, arithmetic and copies ran while one was open for 7% -> 11% of each run, Pallas kernels for 0% -> 0%
where the time goes in v1:
time: 237 us; the launch traced here: 236 us
  waiting for transfers between devices  150 us (63%)
  matrix products  49.4 us (21%)
  between operations  14.3 us (6%)
  starting transfers between devices  14.2 us (6%)
  local copies, waits for them, and re-layouts  5.17 us (2%)
  other arithmetic  3.43 us (1%)
    ppermute x6, waiting for transfers between devices, passed_along(): return lax.ppermute(block, axis, route)  51.4 us
    reduce_scatter x3, waiting for transfers between devices, local(): lax.psum_scatter(row_term(jnp.int32(0), own_cols * lax.axis_size('col')),...  33.2 us
    all_gather x1, waiting for transfers between devices, local(): lax.all_gather(pending, ('tm', 'col'))  33 us
    all_gather x3, waiting for transfers between devices, local(): whole_solved = lax.all_gather(solved, 'col', axis=0, tiled=True)  32 us
    dot_general x3, matrix products, row_term(): jnp.dot(inverse_here, input_rows, precision=highest, preferred_element_ty...  16.7 us
    dot_general x3, matrix products, local(): jnp.dot(upper_masked.T, whole_solved, precision=highest, preferred_elemen...  15.2 us
    dot_general x3, matrix products, local(): jnp.dot(lower_masked.T, whole_solved, precision=highest, preferred_elemen...  15.1 us
    ppermute x6, starting transfers between devices, passed_along(): return lax.ppermute(block, axis, route)  13.9 us
  transfers between devices with their start and end apart: 13, of which 13 were waited for; matrix products, arithmetic and copies ran while one was open for 11% of the time, Pallas kernels for 0%

profile of v1, /device:TPU:1, one launch (start us, length us, event | category | flops | bytes accessed | tf_op | source)
XLA Modules:
  0.0 236.2 jit_solution(10820615355273425218)
XLA Ops:
  7.2 4.5 %fusion.21 = f32[1024,256]{1,0:T(8,128)} fusion(f32[3,1,1024,512]{3,2,1,0:T(8,128)} %param.8, f32[1,512,256]{2,1,0:T(8,128)} %param.7), kind=kOutput, calls=%fused_computation.27 | convolution fusion | flops 1610612736 | bytes 3670016 | tf_op jit(solution)/shard_map/dot_general | solution.py:40
  11.8 11.0 %reduce-scatter.4.cloned.1.call-done = f32[512,256]{1,0:T(8,128)} async-done(((f32[1024,256]{1,0:T(8,128)}), f32[512,256]{1,0:T(8,128)}) %reduce-scatter.4.cloned.1.call-update) | async-done | bytes 524304 | tf_op jit(solution)/shard_map/reduce_scatter | solution.py:44
  23.0 11.5 %all-gather.6.cloned.1.call-done = f32[1024,256]{1,0:T(8,128)} async-done(((f32[512,256]{1,0:T(8,128)}), f32[1024,256]{1,0:T(8,128)}) %all-gather.6.cloned.1.call-update) | async-done | bytes 1048592 | tf_op jit(solution)/shard_map/all_gather | solution.py:50
  35.8 5.1 %fusion.10 = f32[512,256]{1,0:T(8,128)S(1)} fusion(f32[1024,256]{1,0:T(8,128)S(1)} %copy-done.1, f32[128,8,4,128]{3,2,1,0:T(4,128)S(1)} %bitcast.122, f32[3,1,1024,512]{3,2,1,0:T(8,128)} %param.9), kind=kOutput, calls=%fused_computation.16 | convolution fusion | flops 1611137024 | bytes 5767168 | tf_op jit(solution)/shard_map/dot_general | solution.py:51
  40.8 5.3 %collective-permute-start = (f32[512,256]{1,0:T(8,128)S(1)}, f32[512,256]{1,0:T(8,128)S(1)}, u32[]{:S(2)}, u32[]{:S(2)}) collective-permute-start(f32[512,256]{1,0:T(8,128)S(1)} %fusion.10), channel_id=1, source_target_pairs={{2,0},{4,2},{6,4},{8,6},{10,8},{12,10},{14,12},{16,14},{18,16},{20... | collective-permute-start | bytes 1572872 | tf_op jit(solution)/shard_map/ppermute | solution.py:10
  46.4 5.1 %fusion.8 = f32[512,256]{1,0:T(8,128)S(1)} fusion(f32[1024,256]{1,0:T(8,128)S(1)} %copy-done.1, f32[128,8,4,128]{3,2,1,0:T(4,128)S(1)} %bitcast.119, f32[3,1,1024,512]{3,2,1,0:T(8,128)} %param.10), kind=kOutput, calls=%fused_computation.13 | convolution fusion | flops 1611137024 | bytes 5767168 | tf_op jit(solution)/shard_map/dot_general | solution.py:54
  51.8 5.3 %collective-permute-done = f32[512,256]{1,0:T(8,128)S(1)} collective-permute-done((f32[512,256]{1,0:T(8,128)S(1)}, f32[512,256]{1,0:T(8,128)S(1)}, u32[]{:S(2)}, u32[]{:S(2)}) %collective-permute-start) | collective-permute-done | bytes 524320 | tf_op jit(solution)/shard_map/ppermute | solution.py:10
  57.1 11.2 %collective-permute-done.1 = f32[512,256]{1,0:T(8,128)S(1)} collective-permute-done((f32[512,256]{1,0:T(8,128)S(1)}, f32[512,256]{1,0:T(8,128)S(1)}, u32[]{:S(2)}, u32[]{:S(2)}) %collective-permute-start.1) | collective-permute-done | bytes 524320 | tf_op jit(solution)/shard_map/ppermute | solution.py:10
  68.5 6.1 %fusion.33 = f32[1024,256]{0,1:T(8,128)} fusion(f32[512,256]{1,0:T(8,128)S(1)} %fusion.41, f32[3,1,1024,512]{3,2,1,0:T(8,128)} %param.8), kind=kOutput, calls=%fused_computation.39 | convolution fusion | flops 1610612736 | bytes 3670016 | tf_op jit(solution)/shard_map/dot_general | solution.py:40
  74.7 10.2 %reduce-scatter.6.cloned.1.call-done = f32[512,256]{0,1:T(8,128)} async-done(((f32[1024,256]{0,1:T(8,128)}), f32[512,256]{0,1:T(8,128)}) %reduce-scatter.6.cloned.1.call-update) | async-done | bytes 524304 | tf_op jit(solution)/shard_map/reduce_scatter | solution.py:44
  85.1 11.4 %all-gather.8.cloned.1.call-done = f32[1024,256]{0,1:T(8,128)} async-done(((f32[512,256]{0,1:T(8,128)}), f32[1024,256]{0,1:T(8,128)}) %all-gather.8.cloned.1.call-update) | async-done | bytes 1048592 | tf_op jit(solution)/shard_map/all_gather | solution.py:50
  97.8 5.0 %fusion.6 = f32[512,256]{1,0:T(8,128)S(1)} fusion(f32[1024,256]{0,1:T(8,128)S(1)} %copy-done.2, f32[128,8,4,128]{3,2,1,0:T(4,128)S(1)} %bitcast.123, f32[3,1,1024,512]{3,2,1,0:T(8,128)} %param.9), kind=kOutput, calls=%fused_computation.10 | convolution fusion | flops 1611137024 | bytes 5767168 | tf_op jit(solution)/shard_map/dot_general | solution.py:51
  102.8 4.4 %collective-permute-start.2 = (f32[512,256]{1,0:T(8,128)S(1)}, f32[512,256]{1,0:T(8,128)S(1)}, u32[]{:S(2)}, u32[]{:S(2)}) collective-permute-start(f32[512,256]{1,0:T(8,128)S(1)} %fusion.6), channel_id=1, source_target_pairs={{4,0},{6,2},{8,4},{10,6},{12,8},{14,10},{16,12},{18,14},{20,16},{2... | collective-permute-start | bytes 1572872 | tf_op jit(solution)/shard_map/ppermute | solution.py:10
  107.5 5.0 %fusion.4 = f32[512,256]{1,0:T(8,128)S(1)} fusion(f32[1024,256]{0,1:T(8,128)S(1)} %copy-done.2, f32[128,8,4,128]{3,2,1,0:T(4,128)S(1)} %bitcast.120, f32[3,1,1024,512]{3,2,1,0:T(8,128)} %param.10), kind=kOutput, calls=%fused_computation.7 | convolution fusion | flops 1611137024 | bytes 5767168 | tf_op jit(solution)/shard_map/dot_general | solution.py:54
  112.9 5.4 %collective-permute-done.2 = f32[512,256]{1,0:T(8,128)S(1)} collective-permute-done((f32[512,256]{1,0:T(8,128)S(1)}, f32[512,256]{1,0:T(8,128)S(1)}, u32[]{:S(2)}, u32[]{:S(2)}) %collective-permute-start.2) | collective-permute-done | bytes 524320 | tf_op jit(solution)/shard_map/ppermute | solution.py:10
  118.2 10.3 %collective-permute-done.3 = f32[512,256]{1,0:T(8,128)S(1)} collective-permute-done((f32[512,256]{1,0:T(8,128)S(1)}, f32[512,256]{1,0:T(8,128)S(1)}, u32[]{:S(2)}, u32[]{:S(2)}) %collective-permute-start.3) | collective-permute-done | bytes 524320 | tf_op jit(solution)/shard_map/ppermute | solution.py:10
  128.5 6.1 %fusion.36 = f32[1024,256]{0,1:T(8,128)} fusion(f32[3,1,1024,512]{3,2,1,0:T(8,128)} %param.8, f32[512,256]{1,0:T(8,128)S(1)} %collective-permute-done.3, f32[512,256]{1,0:T(8,128)S(1)} %fusion.41, f32[512,256]{1,0:T(8,128)S(1)} %collective-permute-done.2), kind=kOutput, calls=%fused_computation.40 | convolution fusion | flops 1610874880 | bytes 4718592 | tf_op jit(solution)/shard_map/dot_general | solution.py:40
  134.7 12.0 %reduce-scatter.8.cloned.1.call-done = f32[512,256]{0,1:T(8,128)} async-done(((f32[1024,256]{0,1:T(8,128)}), f32[512,256]{0,1:T(8,128)}) %reduce-scatter.8.cloned.1.call-update) | async-done | bytes 524304 | tf_op jit(solution)/shard_map/reduce_scatter | solution.py:44
  149.3 9.1 %all-gather.10.cloned.1.call-done = f32[1024,256]{0,1:T(8,128)} async-done(((f32[512,256]{0,1:T(8,128)}), f32[1024,256]{0,1:T(8,128)}) %all-gather.10.cloned.1.call-update) | async-done | bytes 1048592 | tf_op jit(solution)/shard_map/all_gather | solution.py:50
  159.6 5.0 %fusion.2 = f32[512,256]{1,0:T(8,128)S(1)} fusion(f32[1024,256]{0,1:T(8,128)S(1)} %copy-done, f32[128,8,4,128]{3,2,1,0:T(4,128)S(1)} %bitcast.124, f32[3,1,1024,512]{3,2,1,0:T(8,128)} %param.9), kind=kOutput, calls=%fused_computation.4 | convolution fusion | flops 1611137024 | bytes 5767168 | tf_op jit(solution)/shard_map/dot_general | solution.py:51
  168.7 5.0 %fusion = f32[512,256]{1,0:T(8,128)S(1)} fusion(f32[1024,256]{0,1:T(8,128)S(1)} %copy-done, f32[128,8,4,128]{3,2,1,0:T(4,128)S(1)} %bitcast.121, f32[3,1,1024,512]{3,2,1,0:T(8,128)} %param.10), kind=kOutput, calls=%fused_computation.1 | convolution fusion | flops 1611137024 | bytes 5767168 | tf_op jit(solution)/shard_map/dot_general | solution.py:54
  173.8 6.7 %collective-permute-done.4 = f32[512,256]{1,0:T(8,128)S(1)} collective-permute-done((f32[512,256]{1,0:T(8,128)S(1)}, f32[512,256]{1,0:T(8,128)S(1)}, u32[]{:S(2)}, u32[]{:S(2)}) %collective-permute-start.4) | collective-permute-done | bytes 524320 | tf_op jit(solution)/shard_map/ppermute | solution.py:10
  180.6 12.5 %collective-permute-done.5 = f32[512,256]{1,0:T(8,128)S(1)} collective-permute-done((f32[512,256]{1,0:T(8,128)S(1)}, f32[512,256]{1,0:T(8,128)S(1)}, u32[]{:S(2)}, u32[]{:S(2)}) %collective-permute-start.5) | collective-permute-done | bytes 524320 | tf_op jit(solution)/shard_map/ppermute | solution.py:10
  194.0 33.0 %all-gather.12.cloned.1.call-done = f32[2048,256]{1,0:T(8,128)} async-done(((f32[64,256]{1,0:T(8,128)}), f32[2048,256]{1,0:T(8,128)}) %all-gather.12.cloned.1.call-update) | async-done | bytes 2097168 | tf_op jit(solution)/shard_map/all_gather | solution.py:67
  (58 shorter events, 15.5 us)
Async XLA Ops:
  7.2 15.7 %copy-start.9 = (s32[3,1,2,8,4]{3,4,2,1,0:T(4,128)S(1)}, s32[3,1,2,8,4]{3,4,2,1,0:T(4,128)}, u32[]{:S(2)}) copy-start(s32[3,1,2,8,4]{3,4,2,1,0:T(4,128)} %param.11) | copy-start | bytes 2308
  7.2 15.6 %reduce-scatter.4.cloned.1.call-start = ((), (), s32[]{:S(2)}) async-start(), calls=%async_computation.3 | async-start | bytes 1572864 | tf_op jit(solution)/shard_map/reduce_scatter | solution.py:44
  11.7 22.8 %all-gather.6.cloned.1.call-start = ((), (), s32[]{:S(2)}) async-start(), calls=%async_computation.4 | async-start | bytes 1572864 | tf_op jit(solution)/shard_map/all_gather | solution.py:50
  22.8 62.1 %reduce-scatter.6.cloned.1.call-start = ((), (), s32[]{:S(2)}) async-start(), calls=%async_computation.5 | async-start | bytes 1572864 | tf_op jit(solution)/shard_map/reduce_scatter | solution.py:44
  34.5 1.2 copy-start.1
  40.8 16.3 %collective-permute-start = (f32[512,256]{1,0:T(8,128)S(1)}, f32[512,256]{1,0:T(8,128)S(1)}, u32[]{:S(2)}, u32[]{:S(2)}) collective-permute-start(f32[512,256]{1,0:T(8,128)S(1)} %fusion.10), channel_id=1, source_target_pairs={{2,0},{4,2},{6,4},{8,6},{10,8},{12,10},{14,12},{16,14},{18,16},{20... | collective-permute-start | bytes 1572872 | tf_op jit(solution)/shard_map/ppermute | solution.py:10
  46.4 21.9 %copy-start.3 = (f32[1,512,256]{2,1,0:T(8,128)S(1)}, f32[1,512,256]{2,1,0:T(8,128)}, u32[]{:S(2)}) copy-start(f32[1,512,256]{2,1,0:T(8,128)} %param.7) | copy-start | bytes 1572868
  51.6 16.8 %collective-permute-start.1 = (f32[512,256]{1,0:T(8,128)S(1)}, f32[512,256]{1,0:T(8,128)S(1)}, u32[]{:S(2)}, u32[]{:S(2)}) collective-permute-start(f32[512,256]{1,0:T(8,128)S(1)} %fusion.8), channel_id=1, source_target_pairs={{30,0},{0,2},{2,4},{4,6},{6,8},{8,10},{10,12},{12,14},{14,16},{16,... | collective-permute-start | bytes 1572872 | tf_op jit(solution)/shard_map/ppermute | solution.py:10
  74.6 21.9 %all-gather.8.cloned.1.call-start = ((), (), s32[]{:S(2)}) async-start(), calls=%async_computation.6 | async-start | bytes 1572864 | tf_op jit(solution)/shard_map/all_gather | solution.py:50
  84.9 61.9 %reduce-scatter.8.cloned.1.call-start = ((), (), s32[]{:S(2)}) async-start(), calls=%async_computation.7 | async-start | bytes 1572864 | tf_op jit(solution)/shard_map/reduce_scatter | solution.py:44
  96.5 1.2 copy-start.2
  102.8 15.4 %collective-permute-start.2 = (f32[512,256]{1,0:T(8,128)S(1)}, f32[512,256]{1,0:T(8,128)S(1)}, u32[]{:S(2)}, u32[]{:S(2)}) collective-permute-start(f32[512,256]{1,0:T(8,128)S(1)} %fusion.6), channel_id=1, source_target_pairs={{4,0},{6,2},{8,4},{10,6},{12,8},{14,10},{16,12},{18,14},{20,16},{2... | collective-permute-start | bytes 1572872 | tf_op jit(solution)/shard_map/ppermute | solution.py:10
  112.6 34.3 %copy-start.4 = (f32[512,256]{1,0:T(8,128)S(1)}, f32[512,256]{1,0:T(8,128)}, u32[]{:S(2)}) copy-start(f32[512,256]{1,0:T(8,128)} %reduce-scatter.4.cloned.1.call-done) | copy-start | bytes 1572868
  112.6 34.3 %copy-start.7 = (f32[3,1,64,512]{3,2,1,0:T(8,128)S(1)}, f32[3,1,64,512]{3,2,1,0:T(8,128)}, u32[]{:S(2)}) copy-start(f32[3,1,64,512]{3,2,1,0:T(8,128)} %param.12) | copy-start | bytes 1179652
  112.6 16.0 %collective-permute-start.3 = (f32[512,256]{1,0:T(8,128)S(1)}, f32[512,256]{1,0:T(8,128)S(1)}, u32[]{:S(2)}, u32[]{:S(2)}) collective-permute-start(f32[512,256]{1,0:T(8,128)S(1)} %fusion.4), channel_id=1, source_target_pairs={{28,0},{30,2},{0,4},{2,6},{4,8},{6,10},{8,12},{10,14},{12,16},{14,... | collective-permute-start | bytes 1572872 | tf_op jit(solution)/shard_map/ppermute | solution.py:10
  134.7 12.6 %copy-start.5 = (f32[512,256]{0,1:T(8,128)S(1)}, f32[512,256]{0,1:T(8,128)}, u32[]{:S(2)}) copy-start(f32[512,256]{0,1:T(8,128)} %reduce-scatter.6.cloned.1.call-done) | copy-start | bytes 1572868
  134.7 23.7 %all-gather.10.cloned.1.call-start = ((), (), s32[]{:S(2)}) async-start(), calls=%async_computation.8 | async-start | bytes 1572864 | tf_op jit(solution)/shard_map/all_gather | solution.py:50
  146.8 1.1 copy-start.6
  146.8 80.2 %all-gather.12.cloned.1.call-start = ((), (), s32[]{:S(2)}) async-start(), calls=%async_computation.9 | async-start | bytes 2162688 | tf_op jit(solution)/shard_map/all_gather | solution.py:67
  158.4 1.2 copy-start
  164.7 15.9 %collective-permute-start.4 = (f32[512,256]{1,0:T(8,128)S(1)}, f32[512,256]{1,0:T(8,128)S(1)}, u32[]{:S(2)}, u32[]{:S(2)}) collective-permute-start(f32[512,256]{1,0:T(8,128)S(1)} %fusion.2), channel_id=1, source_target_pairs={{8,0},{10,2},{12,4},{14,6},{16,8},{18,10},{20,12},{22,14},{24,16},... | collective-permute-start | bytes 1572872 | tf_op jit(solution)/shard_map/ppermute | solution.py:10
  173.8 54.9 %copy-start.8 = (f32[64,256]{1,0:T(8,128)S(1)}, f32[64,256]{1,0:T(8,128)}, u32[]{:S(2)}) copy-start(f32[64,256]{1,0:T(8,128)} %param.13) | copy-start | bytes 196612
  173.8 19.3 %collective-permute-start.5 = (f32[512,256]{1,0:T(8,128)S(1)}, f32[512,256]{1,0:T(8,128)S(1)}, u32[]{:S(2)}, u32[]{:S(2)}) collective-permute-start(f32[512,256]{1,0:T(8,128)S(1)} %fusion), channel_id=1, source_target_pairs={{24,0},{26,2},{28,4},{30,6},{0,8},{2,10},{4,12},{6,14},{8,16},{10,... | collective-permute-start | bytes 1572872 | tf_op jit(solution)/shard_map/ppermute | solution.py:10
Sparse Core Ops, SparseCore 0:
  11.9 10.8 reduce-scatter.3
  24.3 10.1 all-gather.5
  74.7 10.0 reduce-scatter.5
  86.3 10.2 all-gather.7
  134.8 11.9 reduce-scatter.7
  148.2 10.1 all-gather.9
  161.8 65.1 all-gather.11
